TPU v7x, 32 devices: a whole 2x2x4 slice. The times are simulated.
32 devices in a mesh: dp: 4 (over y, x), ctx: 2 (over core), tp: 4 (over z).
Axes of the slice: x: 2, y: 2, z: 4, core: 2. Of those that a mesh axis runs over, the one named last changes fastest.
Arguments:
- tokens: bfloat16 [4096, 1024], P(('dp', 'ctx')), may hold values from -6 to 6
- norm_gain: float32 [1024], replicated, may hold values from 0.5 to 1.5
- gate_weight: bfloat16 [1024, 2048], P(('dp', 'ctx'), 'tp'), may hold values from -0.1875 to 0.1875
- input_weight: bfloat16 [1024, 2048], P(('dp', 'ctx'), 'tp'), may hold values from -0.1875 to 0.1875
- state_weight: bfloat16 [1024, 256], P(('dp', 'ctx'), 'tp'), may hold values from -0.1875 to 0.1875
- step_weight: bfloat16 [1024, 32], P(('dp', 'ctx'), 'tp'), may hold values from -0.1875 to 0.1875
- input_kernel: float32 [4, 2048], P(None, 'tp'), may hold values from -0.5 to 0.5
- input_offset: float32 [2048], P('tp'), may hold values from -0.5 to 0.5
- state_kernel: float32 [4, 256], P(None, 'tp'), may hold values from -0.5 to 0.5
- state_offset: float32 [256], P('tp'), may hold values from -0.5 to 0.5
- step_bias: float32 [32], P('tp'), may hold values from -5.5 to -3.5
- decay_log: float32 [32], P('tp'), may hold values from -4.6 to 1.1
- skip_gain: float32 [32], P('tp'), may hold values from 0.5 to 1.5
- gated_gain: float32 [2048], P('tp'), may hold values from 0.5 to 1.5
- out_weight: bfloat16 [2048, 1024], P('tp', ('dp', 'ctx')), may hold values from -0.125 to 0.125
- cotangent: bfloat16 [4096, 1024], P(('dp', 'ctx')), may hold values from -6 to 6
Outputs:
- block_out: bfloat16 [4096, 1024], P(('dp', 'ctx'))
- grad_tokens: float32 [4096, 1024], P(('dp', 'ctx'))
- grad_norm_gain: float32 [1024], replicated
- grad_gate_weight: float32 [1024, 2048], P(('dp', 'ctx'), 'tp')
- grad_input_weight: float32 [1024, 2048], P(('dp', 'ctx'), 'tp')
- grad_state_weight: float32 [1024, 256], P(('dp', 'ctx'), 'tp')
- grad_step_weight: float32 [1024, 32], P(('dp', 'ctx'), 'tp')
- grad_input_kernel: float32 [4, 2048], P(None, 'tp')
- grad_input_offset: float32 [2048], P('tp')
- grad_state_kernel: float32 [4, 256], P(None, 'tp')
- grad_state_offset: float32 [256], P('tp')
- grad_step_bias: float32 [32], P('tp')
- grad_decay_log: float32 [32], P('tp')
- grad_skip_gain: float32 [32], P('tp')
- grad_gated_gain: float32 [2048], P('tp')
- grad_out_weight: float32 [2048, 1024], P('tp', ('dp', 'ctx'))
All inputs are finite; a program needn't handle non-finite values.
Results may differ from a plain program's by a relative error of at most 0.012.
Values may be sent and summed in bfloat16 or wider, within the bound.
A program may use at most 128 MiB of HBM per device.

v0:
```python
import functools

import jax
import jax.numpy as jnp
from jax import lax
from jax.experimental import pallas as pl
from jax.experimental.pallas import tpu as pltpu
from jax.sharding import PartitionSpec as P

DI = 2048
STRETCH = 256


epsilon = 1e-05
exact_mode = lax.Precision.HIGHEST


def shifted(value, axis, steps):
    count = lax.axis_size(axis)
    leading, last = (max(0, -steps), min(count, count - steps))
    return lax.ppermute(value, axis, [(source, source + steps) for source in range(leading, last)])


def chained(log_decay, state, axis, combine, backward, ident):
    size, here = (lax.axis_size(axis), lax.axis_index(axis))
    rows, nstate = state.shape
    heads = log_decay.shape[0]
    packed = jnp.concatenate(
        [state, jnp.broadcast_to(log_decay[:, None], (heads, nstate)).astype(state.dtype)]
    )
    everything = spread(packed, axis, size, ident).astype(jnp.float32)
    logs = everything[:, rows:, 0]
    states = everything[:, :rows].reshape(size, heads, rows // heads, nstate)
    before = (jnp.zeros((heads,), jnp.float32), jnp.zeros(states.shape[1:], jnp.float32))
    for k in range(size):
        at = size - 1 - k if backward else k
        reached = at > here if backward else at < here
        new = combine(before, (logs[at], states[at]))
        before = jax.tree.map(lambda a, b: jnp.where(reached, a, b), new, before)
    return before[1].reshape(rows, nstate)


def rms_norm(values, norm_scale):
    meansq = jnp.mean(values * values, axis=-1, keepdims=True)
    return values * lax.rsqrt(meansq + epsilon) * norm_scale


def causal_conv(padded, kernel, offset):
    tap_count = kernel.shape[0]
    length = padded.shape[0] - tap_count + 1
    summed = offset[None, :] + kernel[0][None, :] * padded[0:length]
    for tap_index in range(1, tap_count):
        summed = summed + kernel[tap_index][None, :] * padded[tap_index : tap_index + length]
    return jax.nn.silu(summed)


def forward_chain(earlier, later):
    return (earlier[0] + later[0], jnp.exp(later[0])[:, None, None] * earlier[1] + later[1])


def backward_chain(earlier, later):
    return (earlier[0] + later[0], later[1] + jnp.exp(later[0])[:, None, None] * earlier[1])


def times_transposed(left_side, right_side):
    return lax.dot_general(
        left_side, right_side, (((1,), (1,)), ((), ())), preferred_element_type=jnp.float32
    )


def over_rows(left_side, right_side):
    return lax.dot_general(
        left_side, right_side, (((0,), (0,)), ((), ())), preferred_element_type=jnp.float32
    )


MESH = pl.DeviceIdType.MESH
LANES = 128


def line_up(peers):
    barrier = pltpu.get_barrier_semaphore()
    for peer in peers:
        pl.semaphore_signal(barrier, inc=1, device_id=peer, device_id_type=MESH)
    pl.semaphore_wait(barrier, len(peers))


def send_to(source, target, sends, recvs, peer):
    return pltpu.make_async_remote_copy(
        src_ref=source,
        dst_ref=target,
        send_sem=sends,
        recv_sem=recvs,
        device_id=peer,
        device_id_type=MESH,
    )


def gather_kernel(n, ctxn, x_ref, full_ref, own_sem, send, recv, fsend, frecv):
    here = lax.axis_index("dp") * ctxn + lax.axis_index("ctx")
    half = n // 2
    chip, core = lax.div(here, 2), lax.rem(here, 2)
    rows = x_ref.shape[0]

    def spot(index):
        return {"dp": lax.div(index, ctxn), "ctx": lax.rem(index, ctxn)}

    def at(index):
        return full_ref.at[pl.ds(pl.multiple_of(index * rows, rows), rows)]

    sibling = spot(2 * chip + 1 - core)
    peers = [spot(2 * lax.rem(chip + step, half) + core) for step in range(1, half)]
    line_up([sibling] + peers)
    copies = []
    for step in range(1, half):
        copy = send_to(x_ref, at(here), send.at[step], recv.at[step], peers[step - 1])
        copy.start()
        copies.append(copy)
    beside = send_to(x_ref, at(here), send.at[0], recv.at[0], sibling)
    beside.start()
    own = pltpu.make_async_copy(x_ref, at(here), own_sem)
    own.start()
    passed = []
    for step in range(1, half):
        origin = 2 * lax.rem(chip + half - step, half) + core
        copies[step - 1].wait_recv()
        copy = send_to(at(origin), at(origin), fsend.at[step], frecv.at[step], sibling)
        copy.start()
        passed.append(copy)
    own.wait()
    beside.wait()
    for copy in copies:
        copy.wait_send()
    for copy in passed:
        copy.wait()


def gather_rows(shard, n, ctxn, ident):
    rows, columns = shard.shape
    half = n // 2
    return pl.pallas_call(
        functools.partial(gather_kernel, n, ctxn),
        out_shape=jax.ShapeDtypeStruct((n * rows, columns), shard.dtype),
        in_specs=[pl.BlockSpec(memory_space=pltpu.VMEM)],
        out_specs=pl.BlockSpec(memory_space=pltpu.VMEM),
        scratch_shapes=[pltpu.SemaphoreType.DMA] + [pltpu.SemaphoreType.DMA((half,))] * 4,
        compiler_params=pltpu.CompilerParams(
            collective_id=ident, has_side_effects=True, vmem_limit_bytes=10 * 2**20
        ),
    )(shard)


def spread_kernel(axis, n, x_ref, all_ref, own_sem, send, recv):
    here = lax.axis_index(axis)
    peers = [{axis: lax.rem(here + step, n)} for step in range(1, n)]
    line_up(peers)
    copies = []
    for step in range(1, n):
        copy = send_to(x_ref, all_ref.at[here], send.at[step], recv.at[step], peers[step - 1])
        copy.start()
        copies.append(copy)
    own = pltpu.make_async_copy(x_ref, all_ref.at[here], own_sem)
    own.start()
    own.wait()
    for copy in copies:
        copy.wait()


def spread(array, axis, n, ident):
    return pl.pallas_call(
        functools.partial(spread_kernel, axis, n),
        out_shape=jax.ShapeDtypeStruct((n,) + array.shape, array.dtype),
        in_specs=[pl.BlockSpec(memory_space=pltpu.VMEM)],
        out_specs=pl.BlockSpec(memory_space=pltpu.VMEM),
        scratch_shapes=[pltpu.SemaphoreType.DMA] + [pltpu.SemaphoreType.DMA((n,))] * 2,
        compiler_params=pltpu.CompilerParams(
            collective_id=ident, has_side_effects=True, vmem_limit_bytes=10 * 2**20
        ),
    )(array)


def finish_kernel(
    n,
    ctxn,
    tpn,
    grads_ref,
    part_ref,
    small_ref,
    tokens_ref,
    cot_ref,
    gain_ref,
    dw_ref,
    gt_ref,
    sum_ref,
    total_ref,
    beside_buf,
    out_buf,
    in_buf,
    small_in,
    gain_out,
    gain_in,
    tp_in,
    tp_out,
    tp_all,
    sems,
    small_sems,
    tp_sems,
):
    here = lax.axis_index("dp") * ctxn + lax.axis_index("ctx")
    mine = lax.axis_index("tp")
    half = n // 2
    chip, core = lax.div(here, 2), lax.rem(here, 2)
    rows = dw_ref.shape[0]
    piece = tp_out.shape[0]

    def spot(index):
        return {"dp": lax.div(index, ctxn), "ctx": lax.rem(index, ctxn)}

    def span(index):
        return pl.ds(pl.multiple_of(index * rows, rows), rows)

    def part(index):
        return pl.ds(pl.multiple_of(index * piece, piece), piece)

    sibling = spot(2 * chip + 1 - core)
    group = [spot(lax.rem(here + step, n)) for step in range(1, n)]
    line = [{"tp": lax.rem(mine + step, tpn)} for step in range(1, tpn)]
    line_up(group + line)

    scatter = []
    for step in range(1, tpn):
        copy = send_to(
            part_ref.at[part(lax.rem(mine + step, tpn))],
            tp_in.at[step],
            tp_sems.at[0, step],
            tp_sems.at[1, step],
            line[step - 1],
        )
        copy.start()
        scatter.append(copy)
    beside = []
    for step in list(range(1, half)) + [0]:
        copy = send_to(
            grads_ref.at[span(2 * lax.rem(chip + step, half) + 1 - core)],
            beside_buf.at[step],
            sems.at[0, step],
            sems.at[1, step],
            sibling,
        )
        copy.start()
        beside.append(copy)
    smalls = []
    for step in range(1, n):
        copy = send_to(
            small_ref, small_in.at[here], small_sems.at[0, step], small_sems.at[1, step], group[step - 1]
        )
        copy.start()
        smalls.append(copy)
    small_in[here] = small_ref[...]

    across = []
    for step in range(1, half):
        target = 2 * lax.rem(chip + step, half) + core
        beside[step - 1].wait_recv()
        out_buf[step] = (
            grads_ref[span(target)].astype(jnp.float32) + beside_buf[step].astype(jnp.float32)
        ).astype(jnp.bfloat16)
        copy = send_to(
            out_buf.at[step], in_buf.at[step], sems.at[2, step], sems.at[3, step], spot(target)
        )
        copy.start()
        across.append(copy)
    beside[half - 1].wait_recv()
    dw_ref[...] = grads_ref[span(here)].astype(jnp.float32) + beside_buf[0].astype(jnp.float32)

    for copy in smalls:
        copy.wait_recv()
    total = small_in[0]
    for index in range(1, n):
        total = total + small_in[index]
    sum_ref[...] = total
    gain_out[...] = total[:8]
    gain_in[mine] = total[:8]
    gains = []
    for step in range(1, tpn):
        copy = send_to(
            gain_out, gain_in.at[mine], tp_sems.at[4, step], tp_sems.at[5, step], line[step - 1]
        )
        copy.start()
        gains.append(copy)

    normed_grad = part_ref[part(mine)].astype(jnp.float32)
    for step in range(1, tpn):
        scatter[step - 1].wait_recv()
        normed_grad = normed_grad + tp_in[step].astype(jnp.float32)
    tokens = tokens_ref[part(mine)].astype(jnp.float32)
    inv = lax.rsqrt(jnp.mean(tokens * tokens, axis=-1, keepdims=True) + epsilon)
    scaled = normed_grad * gain_ref[...]
    along = jnp.mean(scaled * tokens, axis=-1, keepdims=True)
    change = (inv * scaled - tokens * (inv * inv * inv * along)).astype(jnp.bfloat16)
    tp_out[...] = change
    collect = []
    for step in range(1, tpn):
        copy = send_to(
            tp_out, tp_all.at[part(mine)], tp_sems.at[2, step], tp_sems.at[3, step], line[step - 1]
        )
        copy.start()
        collect.append(copy)
    gt_ref[part(mine)] = cot_ref[part(mine)].astype(jnp.float32) + change.astype(jnp.float32)

    for step in range(1, half):
        across[step - 1].wait_recv()
        dw_ref[...] += in_buf[step].astype(jnp.float32)
    for copy in gains:
        copy.wait_recv()
    whole = gain_in[0]
    for index in range(1, tpn):
        whole = whole + gain_in[index]
    total_ref[...] = whole
    for step in range(1, tpn):
        collect[step - 1].wait_recv()
        where = part(lax.rem(mine + tpn - step, tpn))
        gt_ref[where] = cot_ref[where].astype(jnp.float32) + tp_all[where].astype(jnp.float32)
    for copy in scatter + beside + smalls + across + gains + collect:
        copy.wait_send()


def finish(grads, part, small, tokens, cotangent, norm_gain, n, ctxn, tpn, ident):
    rows, columns = grads.shape[0] // n, grads.shape[1]
    length, width = tokens.shape
    half = n // 2
    piece = length // tpn
    return pl.pallas_call(
        functools.partial(finish_kernel, n, ctxn, tpn),
        out_shape=(
            jax.ShapeDtypeStruct((rows, columns), jnp.float32),
            jax.ShapeDtypeStruct((length, width), jnp.float32),
            jax.ShapeDtypeStruct(small.shape, jnp.float32),
            jax.ShapeDtypeStruct((8, LANES), jnp.float32),
        ),
        in_specs=[pl.BlockSpec(memory_space=pltpu.VMEM)] * 6,
        out_specs=(pl.BlockSpec(memory_space=pltpu.VMEM),) * 4,
        scratch_shapes=[
            pltpu.VMEM((half, rows, columns), jnp.bfloat16),
            pltpu.VMEM((half, rows, columns), jnp.bfloat16),
            pltpu.VMEM((half, rows, columns), jnp.bfloat16),
            pltpu.VMEM((n,) + small.shape, jnp.float32),
            pltpu.VMEM((8, LANES), jnp.float32),
            pltpu.VMEM((tpn, 8, LANES), jnp.float32),
            pltpu.VMEM((tpn, piece, width), jnp.bfloat16),
            pltpu.VMEM((piece, width), jnp.bfloat16),
            pltpu.VMEM((length, width), jnp.bfloat16),
            pltpu.SemaphoreType.DMA((4, half)),
            pltpu.SemaphoreType.DMA((2, n)),
            pltpu.SemaphoreType.DMA((6, tpn)),
        ],
        compiler_params=pltpu.CompilerParams(
            collective_id=ident, has_side_effects=True, vmem_limit_bytes=28 * 2**20
        ),
    )(grads, part, small, tokens, cotangent, norm_gain.reshape(1, width))


def swap_kernel(axis, n, x_ref, all_ref, own_sem, send, recv):
    here = lax.axis_index(axis)
    peers = [{axis: lax.rem(here + step, n)} for step in range(1, n)]
    line_up(peers)
    copies = []
    for step in range(1, n):
        copy = send_to(
            x_ref.at[lax.rem(here + step, n)],
            all_ref.at[here],
            send.at[step],
            recv.at[step],
            peers[step - 1],
        )
        copy.start()
        copies.append(copy)
    own = pltpu.make_async_copy(x_ref.at[here], all_ref.at[here], own_sem)
    own.start()
    own.wait()
    for copy in copies:
        copy.wait()


def swap(array, axis, n, ident):
    return pl.pallas_call(
        functools.partial(swap_kernel, axis, n),
        out_shape=jax.ShapeDtypeStruct(array.shape, array.dtype),
        in_specs=[pl.BlockSpec(memory_space=pltpu.VMEM)],
        out_specs=pl.BlockSpec(memory_space=pltpu.VMEM),
        scratch_shapes=[pltpu.SemaphoreType.DMA] + [pltpu.SemaphoreType.DMA((n,))] * 2,
        compiler_params=pltpu.CompilerParams(
            collective_id=ident, has_side_effects=True, vmem_limit_bytes=10 * 2**20
        ),
    )(array)


def mm(left, right, dims):
    return lax.dot_general(left, right, (dims, ((), ())), preferred_element_type=jnp.float32)


def widen(columns, width):
    rows, heads = columns.shape
    return jnp.concatenate(
        [jnp.broadcast_to(columns[:, h : h + 1], (rows, width)) for h in range(heads)], axis=1
    )


def tallen(row, width, lanes):
    return jnp.concatenate(
        [jnp.broadcast_to(row[:, h : h + 1], (width, lanes)) for h in range(row.shape[1])], axis=0
    )


def per_head(wide, heads):
    width = wide.shape[1] // heads
    return jnp.concatenate(
        [
            jnp.sum(wide[:, h * width : (h + 1) * width], axis=1, keepdims=True)
            for h in range(heads)
        ],
        axis=1,
    )


def decay_matrix(run, run_row, h, causal):
    return jnp.exp(jnp.where(causal, run[:, h : h + 1] - run_row[h : h + 1, :], -1e30))


def causal_mask(size):
    down = lax.broadcasted_iota(jnp.int32, (size, size), 0)
    right = lax.broadcasted_iota(jnp.int32, (size, size), 1)
    return down >= right


def scan_kernel(
    heads,
    x_ref,
    gate_ref,
    bc_ref,
    run_ref,
    run_row_ref,
    dt_ref,
    dt_row_ref,
    start_ref,
    skip_ref,
    gain_ref,
    scanned_ref,
    scaled_ref,
    square_ref,
    kept_ref,
    state,
):
    low = jnp.bfloat16

    @pl.when(pl.program_id(0) == 0)
    def _():
        state[...] = start_ref[...]

    size, inner = x_ref.shape
    width = inner // heads
    nstate = bc_ref.shape[1] // 2
    b, c = bc_ref[:, :nstate], bc_ref[:, nstate:]
    run, run_row = run_ref[...], run_row_ref[...]
    x = x_ref[...]
    x_low = x.astype(low)
    causal = causal_mask(size)
    scores = mm(c, b, ((1,), (1,)))
    held = state[...].astype(low)
    kept_ref[0] = held
    carried = mm(c, held, ((1,), (1,))) * widen(jnp.exp(run), width)
    within = []
    for h in range(heads):
        mixing = decay_matrix(run, run_row, h, causal) * scores * dt_row_ref[h : h + 1, :]
        within.append(mm(mixing.astype(low), x_low[:, h * width : (h + 1) * width], ((1,), (0,))))
    scanned = carried + jnp.concatenate(within, axis=1) + skip_ref[...] * x
    scanned_ref[...] = scanned
    total = run[size - 1 :, :]
    tail = jnp.exp(total - run) * dt_ref[...]
    fresh = mm((x * widen(tail, width)).astype(low), b, ((0,), (0,)))
    state[...] = tallen(jnp.exp(total), width, nstate) * state[...] + fresh
    gate = gate_ref[...]
    gated = scanned * (gate * jax.nn.sigmoid(gate))
    scaled_ref[...] = (gated * gain_ref[...]).astype(low)
    square_ref[...] = jnp.sum(gated * gated, axis=1, keepdims=True)


def scan_forward(x, gate, bc, run, run_row, dt, dt_row, start, skip, gain, heads):
    length, inner = x.shape
    nstate = bc.shape[1] // 2
    size = STRETCH
    wide = pl.BlockSpec((size, inner), lambda i: (i, 0))
    thin = pl.BlockSpec((size, heads), lambda i: (i, 0))
    flat = pl.BlockSpec((heads, size), lambda i: (0, i))
    row = pl.BlockSpec((1, inner), lambda i: (0, 0))
    return pl.pallas_call(
        functools.partial(scan_kernel, heads),
        grid=(length // size,),
        out_shape=(
            jax.ShapeDtypeStruct((length, inner), jnp.float32),
            jax.ShapeDtypeStruct((length, inner), jnp.bfloat16),
            jax.ShapeDtypeStruct((length, 1), jnp.float32),
            jax.ShapeDtypeStruct((length // size, inner, nstate), jnp.bfloat16),
        ),
        in_specs=[
            wide,
            wide,
            pl.BlockSpec((size, 2 * nstate), lambda i: (i, 0)),
            thin,
            flat,
            thin,
            flat,
            pl.BlockSpec((inner, nstate), lambda i: (0, 0)),
            row,
            row,
        ],
        out_specs=(
            wide,
            wide,
            pl.BlockSpec((size, 1), lambda i: (i, 0)),
            pl.BlockSpec((1, inner, nstate), lambda i: (i, 0, 0)),
        ),
        scratch_shapes=[pltpu.VMEM((inner, nstate), jnp.float32)],
        compiler_params=pltpu.CompilerParams(
            dimension_semantics=("arbitrary",), vmem_limit_bytes=28 * 2**20
        ),
    )(x, gate, bc, run, run_row, dt, dt_row, start, skip, gain)


def back_kernel(
    heads,
    x_ref,
    dy_ref,
    bc_ref,
    run_ref,
    run_row_ref,
    dt_ref,
    dt_row_ref,
    end_ref,
    kept_ref,
    skip_ref,
    dx_ref,
    dbc_ref,
    ddt_ref,
    ddecay_ref,
    state,
):
    low = jnp.bfloat16

    @pl.when(pl.program_id(0) == 0)
    def _():
        state[...] = end_ref[...]

    size, inner = x_ref.shape
    width = inner // heads
    nstate = bc_ref.shape[1] // 2
    b, c = bc_ref[:, :nstate], bc_ref[:, nstate:]
    run, run_row, dt = run_ref[...], run_row_ref[...], dt_ref[...]
    x, dy = x_ref[...], dy_ref[...]
    x_low, dy_low = x.astype(low), dy.astype(low)
    causal = causal_mask(size)
    scores = mm(c, b, ((1,), (1,)))
    held = kept_ref[0]
    ds = state[...]
    ds_low = ds.astype(low)

    grown = widen(jnp.exp(run), width)
    dy_grown = dy * grown
    dy_grown_low = dy_grown.astype(low)
    drun = per_head(dy_grown * mm(c, held, ((1,), (1,))), heads)
    dc = mm(dy_grown_low, held, ((1,), (0,)))
    total = run[size - 1 :, :]
    left = jnp.exp(total - run)
    fade = widen(left, width)
    spare = widen(left * dt, width)
    pulled = mm(b, ds_low, ((1,), (1,)))
    db = mm((x * spare).astype(low), ds_low, ((1,), (0,)))
    tail_grad = per_head(x * fade * pulled, heads)
    out_tail = tail_grad * dt
    drun = drun - out_tail
    shrink = tallen(jnp.exp(total), width, nstate)
    lost = jnp.sum(shrink * ds * held.astype(jnp.float32), axis=1, keepdims=True)
    dtotal = jnp.concatenate(
        [
            jnp.sum(lost[h * width : (h + 1) * width], axis=0, keepdims=True)
            for h in range(heads)
        ],
        axis=1,
    ) + jnp.sum(out_tail, axis=0, keepdims=True)
    state[...] = shrink * ds + mm(dy_grown_low, c, ((0,), (0,)))

    dscores = jnp.zeros((size, size), jnp.float32)
    rows, columns, dx = [], [], []
    for h in range(heads):
        lanes = slice(h * width, (h + 1) * width)
        fall = decay_matrix(run, run_row, h, causal)
        dt_row = dt_row_ref[h : h + 1, :]
        products = mm(dy_low[:, lanes], x_low[:, lanes], ((1,), (1,))) * fall
        dscores = dscores + products * dt_row
        terms = products * scores
        columns.append(jnp.sum(terms, axis=0, keepdims=True))
        rows.append(jnp.sum(terms * dt_row, axis=1, keepdims=True))
        mixing = (fall * scores * dt_row).astype(low)
        dx.append(mm(mixing, dy_low[:, lanes], ((0,), (0,))))
    dx_ref[...] = jnp.concatenate(dx, axis=1) + spare * pulled + skip_ref[...] * dy
    dscores = dscores.astype(low)
    dbc_ref[:, :nstate] = db + mm(dscores, c, ((0,), (0,)))
    dbc_ref[:, nstate:] = dc + mm(dscores, b, ((1,), (0,)))
    column = jnp.concatenate(columns, axis=0).T
    ddt_ref[...] = column + tail_grad
    drun = drun + jnp.concatenate(rows, axis=1) - column * dt
    later = jnp.where(causal, 1.0, 0.0)
    ddecay_ref[...] = dtotal + lax.dot_general(
        later,
        drun,
        (((0,), (0,)), ((), ())),
        precision=exact_mode,
        preferred_element_type=jnp.float32,
    )


def scan_backward(x, dy, bc, run, run_row, dt, dt_row, end, kept, skip, heads):
    length, inner = x.shape
    nstate = bc.shape[1] // 2
    size = STRETCH
    count = length // size
    last = count - 1
    wide = pl.BlockSpec((size, inner), lambda i: (last - i, 0))
    thin = pl.BlockSpec((size, heads), lambda i: (last - i, 0))
    flat = pl.BlockSpec((heads, size), lambda i: (0, last - i))
    both = pl.BlockSpec((size, 2 * nstate), lambda i: (last - i, 0))
    return pl.pallas_call(
        functools.partial(back_kernel, heads),
        grid=(count,),
        out_shape=(
            jax.ShapeDtypeStruct((length, inner), jnp.float32),
            jax.ShapeDtypeStruct((length, 2 * nstate), jnp.float32),
            jax.ShapeDtypeStruct((length, heads), jnp.float32),
            jax.ShapeDtypeStruct((length, heads), jnp.float32),
        ),
        in_specs=[
            wide,
            wide,
            both,
            thin,
            flat,
            thin,
            flat,
            pl.BlockSpec((inner, nstate), lambda i: (0, 0)),
            pl.BlockSpec((1, inner, nstate), lambda i: (last - i, 0, 0)),
            pl.BlockSpec((1, inner), lambda i: (0, 0)),
        ],
        out_specs=(wide, both, thin, thin),
        scratch_shapes=[pltpu.VMEM((inner, nstate), jnp.float32)],
        compiler_params=pltpu.CompilerParams(
            dimension_semantics=("arbitrary",), vmem_limit_bytes=28 * 2**20
        ),
        cost_estimate=pl.CostEstimate(
            flops=40 * 10**9, bytes_accessed=8 * 2**20, transcendentals=2**20
        ),
    )(x, dy, bc, run, run_row, dt, dt_row, end, kept, skip)


def per_device(
    tokens,
    norm_gain,
    gate_weight,
    input_weight,
    state_weight,
    step_weight,
    input_kernel,
    input_offset,
    state_kernel,
    state_offset,
    step_bias,
    decay_log,
    skip_gain,
    gated_gain,
    out_weight,
    cotangent,
):
    ctxn = lax.axis_size("ctx")
    n, tpn = lax.axis_size("dp") * ctxn, lax.axis_size("tp")
    inner, state_width, heads = input_weight.shape[1], state_weight.shape[1], step_weight.shape[1]
    misc_width = -(-(state_width + heads) // LANES) * LANES
    spare = misc_width - state_width - heads
    shard = jnp.concatenate(
        [
            gate_weight,
            input_weight,
            state_weight,
            step_weight,
            jnp.zeros((gate_weight.shape[0], spare), jnp.bfloat16),
            out_weight.T,
        ],
        axis=1,
    )
    full = gather_rows(shard, n, ctxn, 0)
    edges = (0, inner, 2 * inner, 2 * inner + misc_width, 3 * inner + misc_width)
    full_gate, full_input, full_misc, full_out = (
        full[:, low:high] for low, high in zip(edges[:-1], edges[1:])
    )
    residual_in = tokens.astype(jnp.float32)
    normed_low = rms_norm(residual_in, norm_gain).astype(jnp.bfloat16)
    gate_val = jnp.dot(normed_low, full_gate, preferred_element_type=jnp.float32)
    input_pre = jnp.dot(normed_low, full_input, preferred_element_type=jnp.float32)
    misc_pre = jnp.dot(normed_low, full_misc, preferred_element_type=jnp.float32)
    state_pre = misc_pre[:, :state_width]
    step_pre = misc_pre[:, state_width : state_width + heads]
    length = residual_in.shape[0]
    rim_rows = input_kernel.shape[0] - 1
    rim_input, rim_state = shifted(
        (input_pre[length - rim_rows :], state_pre[length - rim_rows :]), "ctx", 1
    )
    values, input_pull = jax.vjp(
        causal_conv, jnp.concatenate([rim_input, input_pre], axis=0), input_kernel, input_offset
    )
    state_act, state_pull = jax.vjp(
        causal_conv, jnp.concatenate([rim_state, state_pre], axis=0), state_kernel, state_offset
    )
    states_all = spread(state_act.astype(jnp.bfloat16), "tp", tpn, 3)
    states_full = jnp.concatenate([states_all[k] for k in range(tpn)], axis=1)
    nstate = states_full.shape[1] // 2
    headdim = inner // heads
    step_sizes = jax.nn.softplus(step_pre + step_bias)
    decays = -step_sizes * jnp.exp(decay_log)
    running = jnp.dot(jnp.tril(jnp.ones((length, length), jnp.float32)), decays, precision=exact_mode)
    starts = jnp.concatenate(
        [jnp.zeros((1, heads), jnp.float32), running[STRETCH - 1 : length - 1 : STRETCH]]
    )
    run = running - jnp.repeat(starts, STRETCH, axis=0)
    run_row, dt_row = run.T, step_sizes.T
    log_decay = running[-1]
    tail = jnp.repeat(jnp.exp(log_decay - running) * step_sizes, headdim, axis=1)
    local_end = over_rows((values * tail).astype(jnp.bfloat16), states_full[:, :nstate])
    incoming = chained(log_decay, local_end, "ctx", forward_chain, False, 4)
    skip_row = jnp.repeat(skip_gain, headdim)[None, :]
    scanned, scaled_low, squares, kept = scan_forward(
        values,
        gate_val,
        states_full,
        run,
        run_row,
        step_sizes,
        dt_row,
        incoming,
        skip_row,
        gated_gain[None, :],
        heads,
    )
    gate_sig = jax.nn.sigmoid(gate_val)
    gate_silu = gate_val * gate_sig
    gated_out = scanned * gate_silu
    partial_out = times_transposed(scaled_low, full_out)
    upstream = cotangent.astype(jnp.float32)
    stats = jnp.stack(
        [squares[:, 0], jnp.sum(upstream * partial_out, axis=1)]
    )
    stats = jnp.sum(spread(stats, "tp", tpn, 1), axis=0)
    projected = lax.psum(partial_out.astype(jnp.bfloat16), "tp").astype(jnp.float32)
    inv_rms = lax.rsqrt(stats[0] / DI + epsilon)
    block_out = (residual_in + inv_rms[:, None] * projected).astype(jnp.bfloat16)
    proj_grad = (inv_rms[:, None] * upstream).astype(jnp.bfloat16)
    rms_grad = -0.5 * inv_rms * inv_rms * inv_rms * stats[1] / DI
    scaled_grad = jnp.dot(proj_grad, full_out, preferred_element_type=jnp.float32)
    grad_gated_gain = jnp.sum(scaled_grad * gated_out, axis=0)
    gated_grad = scaled_grad * gated_gain + 2.0 * rms_grad[:, None] * gated_out
    heads_grad = gated_grad * gate_silu
    gate_grad = gated_grad * scanned * (gate_sig + gate_silu * (1.0 - gate_sig))
    grown = jnp.repeat(jnp.exp(running), headdim, axis=1)
    direct = over_rows((heads_grad * grown).astype(jnp.bfloat16), states_full[:, nstate:])
    chain_grad = chained(log_decay, direct, "ctx", backward_chain, True, 5)
    values_grad, states_grad, step_direct, decays_grad = scan_backward(
        values,
        heads_grad,
        states_full,
        run,
        run_row,
        step_sizes,
        dt_row,
        chain_grad,
        kept,
        skip_row,
        heads,
    )
    skip_grad = jnp.sum(
        jnp.sum(heads_grad * values, axis=0).reshape(heads, headdim), axis=1
    )
    decay_grad = jnp.sum(decays_grad * decays, axis=0)
    step_grad = (step_direct - decays_grad * jnp.exp(decay_log)) * jax.nn.sigmoid(
        step_pre + step_bias
    )
    step_bias_grad = jnp.sum(step_grad, axis=0)
    states_low = states_grad.astype(jnp.bfloat16)
    state_pieces = jnp.stack(
        [states_low[:, k * state_width : (k + 1) * state_width] for k in range(tpn)]
    )
    state_mine = jnp.sum(swap(state_pieces, "tp", tpn, 6).astype(jnp.float32), axis=0)
    input_ext_grad, input_kernel_grad, input_offset_grad = input_pull(values_grad)
    state_ext_grad, state_kernel_grad, state_offset_grad = state_pull(state_mine)
    back_input, back_state = shifted(
        (input_ext_grad[:rim_rows], state_ext_grad[:rim_rows]), "ctx", -1
    )
    input_low = (
        input_ext_grad[rim_rows:] + jnp.pad(back_input, ((length - rim_rows, 0), (0, 0)))
    ).astype(jnp.bfloat16)
    state_low = (
        state_ext_grad[rim_rows:] + jnp.pad(back_state, ((length - rim_rows, 0), (0, 0)))
    ).astype(jnp.bfloat16)
    gate_low = gate_grad.astype(jnp.bfloat16)
    step_low = step_grad.astype(jnp.bfloat16)
    misc_low = jnp.concatenate(
        [state_low, step_low, jnp.zeros((length, spare), jnp.bfloat16)], axis=1
    )
    normed_part = (
        times_transposed(gate_low, full_gate)
        + times_transposed(input_low, full_input)
        + times_transposed(misc_low, full_misc)
    )
    grads = jnp.concatenate(
        [
            over_rows(normed_low, gate_low).astype(jnp.bfloat16),
            over_rows(normed_low, input_low).astype(jnp.bfloat16),
            over_rows(normed_low, misc_low).astype(jnp.bfloat16),
            over_rows(proj_grad, scaled_low).astype(jnp.bfloat16),
        ],
        axis=1,
    )
    inv_in = lax.rsqrt(jnp.mean(residual_in * residual_in, axis=-1, keepdims=True) + epsilon)
    gain_part = jnp.sum(normed_part * (residual_in * inv_in), axis=0)
    pieces = (
        gain_part,
        input_kernel_grad,
        input_offset_grad,
        state_kernel_grad,
        state_offset_grad,
        step_bias_grad,
        decay_grad,
        skip_grad,
        grad_gated_gain,
    )
    count = sum(array.size for array in pieces)
    padded = -(-count // (8 * LANES)) * 8 * LANES
    small = jnp.concatenate(
        [array.reshape(-1) for array in pieces] + [jnp.zeros((padded - count,), jnp.float32)]
    ).reshape(padded // LANES, LANES)
    weight_sums, grad_tokens, small_sum, gain_sum = finish(
        grads,
        normed_part.astype(jnp.bfloat16),
        small,
        tokens,
        cotangent,
        norm_gain,
        n,
        ctxn,
        tpn,
        2,
    )
    small_sum = small_sum.reshape(-1)
    sums, start = [], 0
    for array in pieces:
        sums.append(small_sum[start : start + array.size].reshape(array.shape))
        start += array.size
    misc_start = 2 * inner
    return (
        block_out,
        grad_tokens,
        gain_sum.reshape(-1),
        weight_sums[:, :inner],
        weight_sums[:, inner : 2 * inner],
        weight_sums[:, misc_start : misc_start + state_width],
        weight_sums[:, misc_start + state_width : misc_start + state_width + heads],
        *sums[1:],
        weight_sums[:, edges[3] :].T,
    )


def solution(mesh):
    placed = (
        P(("dp", "ctx"), None),
        P(),
        P(("dp", "ctx"), "tp"),
        P(("dp", "ctx"), "tp"),
        P(("dp", "ctx"), "tp"),
        P(("dp", "ctx"), "tp"),
        P(None, "tp"),
        P("tp"),
        P(None, "tp"),
        P("tp"),
        P("tp"),
        P("tp"),
        P("tp"),
        P("tp"),
        P("tp", ("dp", "ctx")),
        P(("dp", "ctx"), None),
    )
    return jax.shard_map(
        per_device,
        mesh=mesh,
        in_specs=placed,
        out_specs=(
            P(("dp", "ctx"), None),
            P(("dp", "ctx"), None),
            P(),
            P(("dp", "ctx"), "tp"),
            P(("dp", "ctx"), "tp"),
            P(("dp", "ctx"), "tp"),
            P(("dp", "ctx"), "tp"),
            P(None, "tp"),
            P("tp"),
            P(None, "tp"),
            P("tp"),
            P("tp"),
            P("tp"),
            P("tp"),
            P("tp"),
            P("tp", ("dp", "ctx")),
        ),
        check_vma=False,
    )
```

profile of v0, /device:TPU:0, one launch (start us, length us, event | category | flops | bytes accessed | tf_op | source)
XLA Modules:
  0.0 287.3 jit_solution(9465311780254550024)
XLA Ops:
  7.2 1.0 copy.78
  9.9 1.8 concatenate.36.x_ref
  11.7 1.0 copy-done.17
  12.7 25.3 %shard_map.279 = bf16[1024,1664]{1,0:T(8,128)(2,1)S(1)} custom-call(bf16[128,1664]{1,0:T(8,128)(2,1)S(1)} %copy-done.17), custom_call_target="tpu_custom_call" | custom-call | tf_op jit(solution)/shard_map/pallas_call | solution.py:141
  38.9 0.9 copy-done.57
  40.0 2.4 collective-permute-start.1
  42.4 2.0 fusion.25
  44.4 1.3 collective-permute-start
  46.6 1.7 fusion.22.gate_ref
  51.1 1.1 broadcast_in_dim.27
  52.2 2.5 copy.84
  54.7 1.7 copy.106
  57.5 1.1 broadcast_in_dim.31
  58.6 2.6 copy.88
  61.3 2.4 multiply_convert_fusion.5
  63.7 12.6 %shard_map.280 = bf16[4,512,64]{2,1,0:T(8,128)(2,1)S(1)} custom-call(bf16[512,64]{1,0:T(8,128)(2,1)S(1)} %get-tuple-element.108.x_ref), custom_call_target="tpu_custom_call" | custom-call | tf_op jit(solution)/shard_map/pallas_call | solution.py:170
  76.4 0.9 pad_maximum_fusion.6.bc_ref
  77.3 1.6 fusion.15
  80.1 1.6 shard_map.281
  83.0 1.2 fusion.42.start_ref
  84.3 1.2 copy-done.7
  85.5 1.2 copy-done.9
  86.7 0.9 copy-done.21
  87.7 0.9 copy-done.23
  88.6 0.9 copy-done.25
  89.6 3.4 %shard_map.282 = (f32[512,512]{1,0:T(8,128)S(1)}, bf16[512,512]{1,0:T(8,128)(2,1)S(1)}, f32[512,1]{1,0:T(8,128)S(1)}, bf16[2,512,128]{2,1,0:T(8,128)(2,1)S(1)}) custom-call(f32[512,512]{1,0:T(8,128)S(1)} %copy-done.9, f32[512,512]{1,0:T(8,128)S(1)} %copy-done.7, bf16[512,256]{1,0:T(8,128)(2,1)S(1)} %copy-done.21, f32[512,8]{1,0:T(8,128)S(1)} %copy-done.25, ...), custom_call_target="tpu_custom_call" | custom-call | tf_op jit(solution)/shard_map/pallas_call | solution.py:496
  93.1 1.7 fusion.4
  94.8 1.1 reduce.3
  95.9 7.5 %shard_map.283 = f32[4,2,512]{2,1,0:T(2,128)S(1)} custom-call(f32[2,512]{1,0:T(2,128)S(1)} %pad_maximum_fusion.7.x_ref), custom_call_target="tpu_custom_call" | custom-call | tf_op jit(solution)/shard_map/pallas_call | solution.py:170
  103.5 2.1 fusion.16
  105.7 1.7 multiply_reduce_fusion.1
  107.9 1.0 copy-done.11
  109.1 1.6 shard_map.284
  112.0 1.2 fusion.41.end_ref
  113.3 1.2 copy-done.10
  114.5 1.2 copy-done.12
  115.7 0.9 copy-done.22
  116.7 0.9 copy-done.24
  117.6 0.9 copy-done.26
  118.6 0.9 copy-done.37
  119.5 10.1 %shard_map.285 = (f32[512,512]{1,0:T(8,128)S(1)}, f32[512,256]{1,0:T(8,128)S(1)}, f32[512,8]{1,0:T(8,128)S(1)}, f32[512,8]{1,0:T(8,128)S(1)}) custom-call(f32[512,512]{1,0:T(8,128)S(1)} %copy-done.10, f32[512,512]{1,0:T(8,128)S(1)} %copy-done.12, bf16[512,256]{1,0:T(8,128)(2,1)S(1)} %copy-done.22, f32[512,8]{1,0:T(8,128)S(1)} %copy-done.26, ...), custom_call_target="tpu_custom_call" | custom-call | flops 40000000000 | bytes 8388608 | tf_op jit(solution)/shard_map/pallas_call | solution.py:632
  129.6 0.9 multiply_reduce_fusion.4
  131.1 1.5 pad_add_fusion
  133.0 13.2 %shard_map.286 = bf16[4,512,64]{2,1,0:T(8,128)(2,1)S(1)} custom-call(bf16[4,512,64]{2,1,0:T(8,128)(2,1)S(1)} %pad_maximum_fusion.2.x_ref), custom_call_target="tpu_custom_call" | custom-call | tf_op jit(solution)/shard_map/pallas_call | solution.py:386
  148.1 1.8 convolution_convert_fusion
  149.9 2.1 fusion.20
  152.0 1.9 convolution_convert_fusion.2
  154.0 1.3 collective-permute-start.2
  155.3 1.3 collective-permute-start.3
  156.6 1.0 copy.92
  157.6 1.1 copy.93
  158.7 1.0 fusion.77
  160.7 1.1 fusion.39
  161.8 2.8 fusion.44
  165.3 0.9 convolution_convert_fusion.1
  167.1 48.1 %all-reduce.21.cloned.1.call-done = bf16[512,1024]{1,0:T(8,128)(2,1)} async-done(((bf16[512,1024]{1,0:T(8,128)(2,1)}), bf16[512,1024]{1,0:T(8,128)(2,1)}) %all-reduce.21.cloned.1.call-update) | async-done | bytes 1048592 | tf_op jit(solution)/shard_map/psum | solution.py:760
  215.2 5.8 %fusion.3 = (f32[1024]{0:T(1024)S(1)}, bf16[512,1024]{1,0:T(8,128)(2,1)}, bf16[512,1024]{1,0:T(8,128)(2,1)}) fusion(bf16[512,1024]{1,0:T(8,128)(2,1)} %tokens_ref.1, f32[512]{0:T(512)S(1)} %add_rsqrt_fusion, bf16[512,1024]{1,0:T(8,128)(2,1)} %all-reduce.21.cloned.1.call-done, f32[512]{0:T(512)S(1)} %bitcast.108, f32[512,1024]{1,0:T(8,128)} %fusion.44, ...), kind=kOutput, calls=%fused_computation.9 | convolution fusion | flops 543161344 | bytes 10500096 | tf_op jit(solution)/shard_map/dot_general | solution.py:66
  221.1 1.2 copy-done.5
  222.3 1.2 copy-done.6
  223.6 1.2 copy-done.20
  224.8 45.6 %shard_map.287 = (f32[128,1664]{1,0:T(8,128)S(1)}, f32[512,1024]{1,0:T(8,128)S(1)}, f32[40,128]{1,0:T(8,128)S(1)}, f32[8,128]{1,0:T(8,128)S(1)}) custom-call(bf16[1024,1664]{1,0:T(8,128)(2,1)S(1)} %pad_maximum_fusion.grads_ref, bf16[512,1024]{1,0:T(8,128)(2,1)S(1)} %copy-done.6, f32[40,128]{1,0:T(8,128)S(1)} %bitcast.85, bf16[512,1024]{1,0:T(8,128)(2,1)S(1)} %copy-done.5, ...), custom_call_target="tpu_custom_call" | custom-call | tf_op jit(solution)/shard_map/pallas_call | solution.py:333
  270.4 1.3 copy-done.15
  271.8 0.9 slice_bitcast_fusion
  278.5 1.3 copy.112
  (202 shorter events, 23.8 us)
Async XLA Ops:
  7.2 208.0 %all-reduce.21.cloned.1.call-start = ((), (), s32[]{:S(2)}) async-start(), calls=%async_computation | async-start | bytes 2097152 | tf_op jit(solution)/shard_map/psum | solution.py:760
  11.7 1.0 copy-start.17
  12.7 25.3 %copy-start.1 = (bf16[512,1024]{1,0:T(8,128)(2,1)S(1)}, bf16[512,1024]{1,0:T(8,128)(2,1)}, u32[]{:S(2)}) copy-start(bf16[512,1024]{1,0:T(8,128)(2,1)} %tokens_ref.1) | copy-start | bytes 3145732
  12.7 25.6 %copy-start.33 = (f32[1024]{0:T(1024)S(1)}, f32[1024]{0:T(1024)}, u32[]{:S(2)}) copy-start(f32[1024]{0:T(1024)} %param.17) | copy-start | bytes 12292
  38.0 123.7 %copy-start = (bf16[1024,1664]{1,0:T(8,128)(2,1)}, bf16[1024,1664]{1,0:T(8,128)(2,1)S(1)}, u32[]{:S(2)}) copy-start(bf16[1024,1664]{1,0:T(8,128)(2,1)S(1)} %shard_map.279) | copy-start | bytes 10223620
  40.0 5.7 %copy-start.58 = (f32[512,128]{0,1:T(8,128)S(1)}, f32[512,128]{0,1:T(8,128)}, u32[]{:S(2)}) copy-start(f32[512,128]{0,1:T(8,128)} %copy-done.57) | copy-start | bytes 786436
  40.0 6.4 %copy-start.59 = (f32[8]{0:T(128)S(1)}, f32[8]{0:T(128)}, u32[]{:S(2)}) copy-start(f32[8]{0:T(128)} %param.26) | copy-start | bytes 100
  40.0 6.6 %copy-start.2 = (bf16[512,1024]{1,0:T(8,128)(2,1)S(1)}, bf16[512,1024]{1,0:T(8,128)(2,1)}, u32[]{:S(2)}) copy-start(bf16[512,1024]{1,0:T(8,128)(2,1)} %tokens_ref.1) | copy-start | bytes 3145732
  40.0 21.3 %collective-permute-start.1 = (f32[3,64]{1,0:T(4,128)S(1)}, f32[3,64]{1,0:T(4,128)S(1)}, u32[]{:S(2)}, u32[]{:S(2)}) collective-permute-start(f32[3,64]{1,0:T(4,128)S(1)} %copy.105), channel_id=1, source_target_pairs={{0,4},{1,5},{2,6},{3,7},{8,12},{9,13},{10,14},{11,15},{16,20},{17,... | collective-permute-start | bytes 2312 | tf_op jit(solution)/shard_map/ppermute | solution.py:21
  44.4 2.0 copy-start.41
  44.4 32.9 %collective-permute-start = (f32[3,512]{1,0:T(4,128)S(1)}, f32[3,512]{1,0:T(4,128)S(1)}, u32[]{:S(2)}, u32[]{:S(2)}) collective-permute-start(f32[3,512]{1,0:T(4,128)S(1)} %slice.268), channel_id=1, source_target_pairs={{0,4},{1,5},{2,6},{3,7},{8,12},{9,13},{10,14},{11,15},{16,20},{17,... | collective-permute-start | bytes 18440 | tf_op jit(solution)/shard_map/ppermute | solution.py:21
  46.6 1.8 copy-start.65
  49.2 5.5 %copy-start.61 = (f32[4,64]{1,0:T(4,128)S(1)}, f32[4,64]{1,0:T(4,128)}, u32[]{:S(2)}) copy-start(f32[4,64]{1,0:T(4,128)} %param.24) | copy-start | bytes 3076
  49.2 5.5 %copy-start.60 = (f32[4,512]{1,0:T(4,128)S(1)}, f32[4,512]{1,0:T(4,128)}, u32[]{:S(2)}) copy-start(f32[4,512]{1,0:T(4,128)} %param.22) | copy-start | bytes 24580
  49.9 7.5 %copy-start.63 = (f32[8]{0:T(128)S(1)}, f32[8]{0:T(128)}, u32[]{:S(2)}) copy-start(f32[8]{0:T(128)} %param.28) | copy-start | bytes 100
  54.7 6.6 %copy-start.64 = (f32[64]{0:T(128)S(1)}, f32[64]{0:T(128)}, u32[]{:S(2)}) copy-start(f32[64]{0:T(128)} %param.25) | copy-start | bytes 772
  61.2 16.1 %copy-start.42 = (f32[512,512]{1,0:T(8,128)S(1)}, f32[512,512]{1,0:T(8,128)}, u32[]{:S(2)}) copy-start(f32[512,512]{1,0:T(8,128)} %copy-done.41) | copy-start | bytes 3145732
  61.2 16.1 %copy-start.62 = (f32[512]{0:T(512)S(1)}, f32[512]{0:T(512)}, u32[]{:S(2)}) copy-start(f32[512]{0:T(512)} %param.23) | copy-start | bytes 6148
  76.4 1.0 copy-start.48
  76.4 2.6 copy-start.52
  79.0 1.0 copy-start.38
  80.0 4.3 %copy-start.32 = (f32[512]{0:T(512)S(1)}, f32[512]{0:T(512)}, u32[]{:S(2)}) copy-start(f32[512]{0:T(512)} %param.29) | copy-start | bytes 6148
  84.3 1.2 copy-start.7
  85.5 1.2 copy-start.9
  86.7 0.9 copy-start.21
  87.7 0.9 copy-start.23
  88.6 0.9 copy-start.25
  89.6 3.5 %copy-start.18 = (bf16[512,1024]{1,0:T(8,128)(2,1)S(1)}, bf16[512,1024]{1,0:T(8,128)(2,1)}, u32[]{:S(2)}) copy-start(bf16[512,1024]{1,0:T(8,128)(2,1)} %cot_ref.1) | copy-start | bytes 3145732
  93.0 1.8 copy-start.27
  93.0 1.8 copy-start.31
  93.0 1.8 copy-start.34
  93.0 1.8 copy-start.36
  103.5 2.2 copy-start.8
  103.5 2.2 copy-start.28
  103.5 2.2 copy-start.39
  105.7 1.8 copy-start.45
  105.7 1.8 copy-start.49
  105.7 1.8 copy-start.51
  107.9 1.0 copy-start.11
  113.2 1.2 copy-start.10
  114.5 1.2 copy-start.12
  115.7 0.9 copy-start.22
  116.6 0.9 copy-start.24
  117.6 0.9 copy-start.26
  119.5 10.1 %copy-start.40 = (f32[512,512]{1,0:T(8,128)S(1)}, f32[512,512]{1,0:T(8,128)}, u32[]{:S(2)}) copy-start(f32[512,512]{1,0:T(8,128)} %copy-done.38) | copy-start | bytes 3145732
  119.5 10.1 %copy-start.43 = (f32[512,512]{1,0:T(8,128)S(1)}, f32[512,512]{1,0:T(8,128)}, u32[]{:S(2)}) copy-start(f32[512,512]{1,0:T(8,128)} %copy-done.41) | copy-start | bytes 3145732
  132.7 13.6 %copy-start.46 = (f32[512,64]{1,0:T(8,128)S(1)}, f32[512,64]{1,0:T(8,128)}, u32[]{:S(2)}) copy-start(f32[512,64]{1,0:T(8,128)} %copy.106) | copy-start | bytes 393220
  132.7 13.6 %copy-start.53 = (f32[512,64]{1,0:T(8,128)S(1)}, f32[512,64]{1,0:T(8,128)}, u32[]{:S(2)}) copy-start(f32[512,64]{1,0:T(8,128)} %get-tuple-element.109) | copy-start | bytes 393220
  146.6 1.3 copy-start.19
  146.6 1.4 copy-start.35
  148.1 1.8 copy-start.47
  149.9 2.1 copy-start.3
  154.0 11.3 %collective-permute-start.2 = (f32[3,512]{1,0:T(4,128)S(1)}, f32[3,512]{1,0:T(4,128)S(1)}, u32[]{:S(2)}, u32[]{:S(2)}) collective-permute-start(f32[3,512]{1,0:T(4,128)S(1)} %pad_add_fusion.2), channel_id=1, source_target_pairs={{4,0},{5,1},{6,2},{7,3},{12,8},{13,9},{14,10},{15,11},{20,16},{21,... | collective-permute-start | bytes 18440 | tf_op jit(solution)/shard_map/ppermute | solution.py:21
  155.3 5.4 %collective-permute-start.3 = (f32[3,64]{1,0:T(4,128)S(1)}, f32[3,64]{1,0:T(4,128)S(1)}, u32[]{:S(2)}, u32[]{:S(2)}) collective-permute-start(f32[3,64]{1,0:T(4,128)S(1)} %pad_add_fusion.3), channel_id=1, source_target_pairs={{4,0},{5,1},{6,2},{7,3},{12,8},{13,9},{14,10},{15,11},{20,16},{21,... | collective-permute-start | bytes 2312 | tf_op jit(solution)/shard_map/ppermute | solution.py:21
  160.7 3.9 %copy-start.4 = (bf16[512,1024]{1,0:T(8,128)(2,1)S(1)}, bf16[512,1024]{1,0:T(8,128)(2,1)}, u32[]{:S(2)}) copy-start(bf16[512,1024]{1,0:T(8,128)(2,1)} %tokens_ref.1) | copy-start | bytes 3145732
  160.7 3.9 %copy-start.56 = (bf16[512,8]{1,0:T(8,128)(2,1)S(1)}, bf16[512,8]{1,0:T(8,128)(2,1)}, u32[]{:S(2)}) copy-start(bf16[512,8]{1,0:T(8,128)(2,1)} %copy.94) | copy-start | bytes 24580
  161.8 3.6 %copy-start.44 = (f32[515,512]{1,0:T(8,128)S(1)}, f32[515,512]{1,0:T(8,128)}, u32[]{:S(2)}) copy-start(f32[515,512]{1,0:T(8,128)} %pad_add_fusion) | copy-start | bytes 3164164
  165.3 1.2 copy-start.54
  165.3 1.5 copy-start.55
  221.1 1.2 copy-start.5
  222.3 1.2 copy-start.6
  223.6 1.2 copy-start.20
  270.4 1.3 copy-start.15
  271.7 6.8 %copy-start.16 = (f32[512,1024]{1,0:T(8,128)S(1)}, f32[512,1024]{1,0:T(8,128)}, u32[]{:S(2)}) copy-start(f32[512,1024]{1,0:T(8,128)} %copy-done.15) | copy-start | bytes 6291460
  (7 other events, 6.3 us)
Sparse Core Ops, SparseCore 0:
  160.6 54.5 all-reduce.20
where the time goes:
time: 293 us; the launch traced here: 287 us
  Pallas kernels  121 us (41%)
  local copies, waits for them, and re-layouts  52.1 us (18%)
  waiting for transfers between devices  48.1 us (16%)
  matrix products  25.7 us (9%)
  other arithmetic  19.1 us (7%)
  between operations  14.9 us (5%)
  starting transfers between devices  6.33 us (2%)
    psum x1, waiting for transfers between devices, per_device(): lax.psum(partial_out.astype(jnp.bfloat16), 'tp').astype(jnp.float32)  48.1 us
    pallas_call x1, Pallas kernels, finish(): pl.pallas_call(functools.partial(finish_kernel, n, ctxn, tpn), out_shape=...  45.6 us
    unnamed x144, local copies, waits for them, and re-layouts  31.5 us
    pallas_call x1, Pallas kernels, gather_rows(): pl.pallas_call(functools.partial(gather_kernel, n, ctxn), out_shape=jax.S...  25.3 us
    pallas_call x4, Pallas kernels, spread(): pl.pallas_call(functools.partial(spread_kernel, axis, n), out_shape=jax.S...  23.4 us
    pallas_call x1, Pallas kernels, swap(): pl.pallas_call(functools.partial(swap_kernel, axis, n), out_shape=jax.Sha...  13.2 us
    dot_general x4, matrix products, times_transposed(): lax.dot_general(left_side, right_side, (((1,), (1,)), ((), ())), preferre...  12.4 us
    pallas_call x1, Pallas kernels, scan_backward(): pl.pallas_call(functools.partial(back_kernel, heads), grid=(count,), out_...  10.1 us
  transfers between devices with their start and end apart: 5, of which 1 were waited for; matrix products, arithmetic and copies ran while one was open for 11% of the time, Pallas kernels for 4%

commit v1 on v0

--- a/solution.py
+++ b/solution.py
@@ -718,8 +718,21 @@
     state_act, state_pull = jax.vjp(
         causal_conv, jnp.concatenate([rim_state, state_pre], axis=0), state_kernel, state_offset
     )
-    states_all = spread(state_act.astype(jnp.bfloat16), "tp", tpn, 3)
-    states_full = jnp.concatenate([states_all[k] for k in range(tpn)], axis=1)
+    half_length = length // 2
+    state_low_act = state_act.astype(jnp.bfloat16)
+    states_all = spread(
+        jnp.concatenate([state_low_act[:half_length], state_low_act[half_length:]], axis=1),
+        "tp",
+        tpn,
+        3,
+    )
+    states_full = jnp.concatenate(
+        [
+            jnp.concatenate([states_all[k, :, low:high] for k in range(tpn)], axis=1)
+            for low, high in ((0, state_width), (state_width, 2 * state_width))
+        ],
+        axis=0,
+    )
     nstate = states_full.shape[1] // 2
     headdim = inner // heads
     step_sizes = jax.nn.softplus(step_pre + step_bias)
@@ -731,7 +744,13 @@
     run = running - jnp.repeat(starts, STRETCH, axis=0)
     run_row, dt_row = run.T, step_sizes.T
     log_decay = running[-1]
-    tail = jnp.repeat(jnp.exp(log_decay - running) * step_sizes, headdim, axis=1)
+    members = jnp.where(
+        lax.broadcasted_iota(jnp.int32, (heads, inner), 1) // headdim
+        == lax.broadcasted_iota(jnp.int32, (heads, inner), 0),
+        1.0,
+        0.0,
+    )
+    tail = jnp.dot(jnp.exp(log_decay - running) * step_sizes, members, precision=exact_mode)
     local_end = over_rows((values * tail).astype(jnp.bfloat16), states_full[:, :nstate])
     incoming = chained(log_decay, local_end, "ctx", forward_chain, False, 4)
     skip_row = jnp.repeat(skip_gain, headdim)[None, :]
@@ -757,9 +776,16 @@
         [squares[:, 0], jnp.sum(upstream * partial_out, axis=1)]
     )
     stats = jnp.sum(spread(stats, "tp", tpn, 1), axis=0)
-    projected = lax.psum(partial_out.astype(jnp.bfloat16), "tp").astype(jnp.float32)
+    projected = lax.psum_scatter(
+        partial_out.astype(jnp.bfloat16), "tp", scatter_dimension=0, tiled=True
+    ).astype(jnp.float32)
     inv_rms = lax.rsqrt(stats[0] / DI + epsilon)
-    block_out = (residual_in + inv_rms[:, None] * projected).astype(jnp.bfloat16)
+    piece = length // tpn
+    first = lax.axis_index("tp") * piece
+    block_piece = (
+        lax.dynamic_slice_in_dim(tokens, first, piece).astype(jnp.float32)
+        + lax.dynamic_slice_in_dim(inv_rms, first, piece)[:, None] * projected
+    ).astype(jnp.bfloat16)
     proj_grad = (inv_rms[:, None] * upstream).astype(jnp.bfloat16)
     rms_grad = -0.5 * inv_rms * inv_rms * inv_rms * stats[1] / DI
     scaled_grad = jnp.dot(proj_grad, full_out, preferred_element_type=jnp.float32)
@@ -767,7 +793,7 @@
     gated_grad = scaled_grad * gated_gain + 2.0 * rms_grad[:, None] * gated_out
     heads_grad = gated_grad * gate_silu
     gate_grad = gated_grad * scanned * (gate_sig + gate_silu * (1.0 - gate_sig))
-    grown = jnp.repeat(jnp.exp(running), headdim, axis=1)
+    grown = jnp.dot(jnp.exp(running), members, precision=exact_mode)
     direct = over_rows((heads_grad * grown).astype(jnp.bfloat16), states_full[:, nstate:])
     chain_grad = chained(log_decay, direct, "ctx", backward_chain, True, 5)
     values_grad, states_grad, step_direct, decays_grad = scan_backward(
@@ -791,11 +817,19 @@
         step_pre + step_bias
     )
     step_bias_grad = jnp.sum(step_grad, axis=0)
+    states_grad, block_piece = lax.optimization_barrier((states_grad, block_piece))
+    block_out = lax.all_gather(block_piece, "tp", axis=0, tiled=True)
     states_low = states_grad.astype(jnp.bfloat16)
     state_pieces = jnp.stack(
-        [states_low[:, k * state_width : (k + 1) * state_width] for k in range(tpn)]
-    )
-    state_mine = jnp.sum(swap(state_pieces, "tp", tpn, 6).astype(jnp.float32), axis=0)
+        [
+            jnp.concatenate([owned[:half_length], owned[half_length:]], axis=1)
+            for owned in (
+                states_low[:, k * state_width : (k + 1) * state_width] for k in range(tpn)
+            )
+        ]
+    )
+    state_sum = jnp.sum(swap(state_pieces, "tp", tpn, 6).astype(jnp.float32), axis=0)
+    state_mine = jnp.concatenate([state_sum[:, :state_width], state_sum[:, state_width:]], axis=0)
     input_ext_grad, input_kernel_grad, input_offset_grad = input_pull(values_grad)
     state_ext_grad, state_kernel_grad, state_offset_grad = state_pull(state_mine)
     back_input, back_state = shifted(

time: 293 us -> 242 us (0.83)
  waiting for transfers between devices: 48.1 us -> 1.66 us
  local copies, waits for them, and re-layouts: 52.1 us -> 35.5 us
  Pallas kernels: 121 us -> 128 us
  matrix products: 25.7 us -> 28.9 us
  other arithmetic: 19.1 us -> 22.1 us
    psum x1 -> x0, waiting for transfers between devices: 48.1 us -> none  [per_device(): lax.psum(partial_out.astype(jnp.bfloat16), 'tp').astype(jnp.float32)]
    pallas_call x1, Pallas kernels: 45.6 us -> 61.5 us  [finish(): pl.pallas_call(functools.partial(finish_kernel, n, ctxn, tpn), out_shape=...]
    unnamed x144 -> x121, local copies, waits for them, and re-layouts: 31.5 us -> 23.5 us
    pallas_call x4, Pallas kernels: 23.4 us -> 18 us  [spread(): pl.pallas_call(functools.partial(spread_kernel, axis, n), out_shape=jax.S...]
    reshape x2 -> x0, local copies, waits for them, and re-layouts: 5.13 us -> none  [the longest x1 2.6 us: per_device(): grown = jnp.repeat(jnp.exp(running), headdim, axis=1)]
    pallas_call x1, Pallas kernels: 13.2 us -> 9.7 us  [swap(): pl.pallas_call(functools.partial(swap_kernel, axis, n), out_shape=jax.Sha...]
    reduce_sum x2, other arithmetic: 1.17 us -> 4.31 us  [causal_conv(): kernel[tap_index][None, :] * padded[tap_index:tap_index + length]]
  transfers between devices with their start and end apart: 5 -> 6, of which waited for: 1 -> 1; matrix products, arithmetic and copies ran while one was open for 11% -> 20% of each run, Pallas kernels for 4% -> 34%
where the time goes in v1:
time: 242 us; the launch traced here: 238 us
  Pallas kernels  128 us (53%)
  local copies, waits for them, and re-layouts  35.5 us (15%)
  matrix products  28.9 us (12%)
  other arithmetic  22.1 us (9%)
  between operations  15.1 us (6%)
  starting transfers between devices  6.77 us (3%)
    pallas_call x1, Pallas kernels, finish(): pl.pallas_call(functools.partial(finish_kernel, n, ctxn, tpn), out_shape=...  61.5 us
    pallas_call x1, Pallas kernels, gather_rows(): pl.pallas_call(functools.partial(gather_kernel, n, ctxn), out_shape=jax.S...  25.4 us
    unnamed x121, local copies, waits for them, and re-layouts  23.5 us
    pallas_call x4, Pallas kernels, spread(): pl.pallas_call(functools.partial(spread_kernel, axis, n), out_shape=jax.S...  18 us
    dot_general x4, matrix products, times_transposed(): lax.dot_general(left_side, right_side, (((1,), (1,)), ((), ())), preferre...  10.9 us
    pallas_call x1, Pallas kernels, scan_backward(): pl.pallas_call(functools.partial(back_kernel, heads), grid=(count,), out_...  9.87 us
    pallas_call x1, Pallas kernels, swap(): pl.pallas_call(functools.partial(swap_kernel, axis, n), out_shape=jax.Sha...  9.7 us
    dot_general x6, matrix products, over_rows(): lax.dot_general(left_side, right_side, (((0,), (0,)), ((), ())), preferre...  8.1 us
  transfers between devices with their start and end apart: 6, of which 1 were waited for; matrix products, arithmetic and copies ran while one was open for 20% of the time, Pallas kernels for 34%

profile of v1, /device:TPU:0, one launch (start us, length us, event | category | flops | bytes accessed | tf_op | source)
XLA Modules:
  0.0 237.8 jit_solution(15090314623261282421)
XLA Ops:
  7.2 1.0 copy.74
  8.2 0.8 copy.75
  9.1 0.8 copy.76
  9.9 1.1 concatenate.54.x_ref
  11.0 25.4 %shard_map.279 = bf16[1024,1664]{1,0:T(8,128)(2,1)S(1)} custom-call(bf16[128,1664]{1,0:T(8,128)(2,1)S(1)} %concatenate.54.x_ref), custom_call_target="tpu_custom_call" | custom-call | tf_op jit(solution)/shard_map/pallas_call | solution.py:141
  36.7 1.4 copy-done.1
  38.8 2.4 %collective-permute-start.1 = (f32[3,64]{1,0:T(4,128)S(1)}, f32[3,64]{1,0:T(4,128)S(1)}, u32[]{:S(2)}, u32[]{:S(2)}) collective-permute-start(f32[3,64]{1,0:T(4,128)S(1)} %copy.99), channel_id=1, source_target_pairs={{0,4},{1,5},{2,6},{3,7},{8,12},{9,13},{10,14},{11,15},{16,20},{17,... | collective-permute-start | bytes 2312 | tf_op jit(solution)/shard_map/ppermute | solution.py:21
  41.2 2.0 fusion.26
  43.2 1.3 collective-permute-start
  44.9 2.1 fusion.23.gate_ref
  47.2 0.9 copy.81.dt_ref
  49.1 0.8 copy.80.run_ref
  50.7 0.9 multiply_convert_fusion.1
  51.7 8.6 %shard_map.280 = bf16[4,256,128]{2,1,0:T(8,128)(2,1)S(1)} custom-call(bf16[256,128]{1,0:T(8,128)(2,1)S(1)} %pad_maximum_fusion.7.x_ref), custom_call_target="tpu_custom_call" | custom-call | tf_op jit(solution)/shard_map/pallas_call | solution.py:170
  60.7 4.2 %fusion.16 = (f32[512,512]{1,0:T(8,128)S(1)}, f32[512,512]{1,0:T(8,128)}) fusion(f32[512,512]{1,0:T(8,128)} %copy-done.29, f32[512]{0:T(512)S(1)} %bitcast.109, f32[3,512]{1,0:T(4,128)S(1)} %collective-permute-done, f32[512]{0:T(512)S(1)} %bitcast.111, f32[512]{0:T(512)S(1)} %bitcast.107, f32[512]{0:T(512)S(1)} %bitcast.105, f32[512]{0:T(512)} %param.23), kind=kLoop, calls=%fused_computation.45 | loop fusion | flops 3932160 | bytes 3162112 | tf_op jit(solution)/shard_map/jvp(jit(silu))/mul | solution.py:54
  64.9 1.1 fusion.7
  66.5 1.6 shard_map.281
  68.1 0.8 copy-done.4
  69.4 1.3 fusion.41.start_ref
  70.7 0.9 copy-done.10
  71.6 0.9 copy-done.12
  72.6 3.4 %shard_map.282 = (f32[512,512]{1,0:T(8,128)S(1)}, bf16[512,512]{1,0:T(8,128)(2,1)S(1)}, f32[512,1]{1,0:T(8,128)S(1)}, bf16[2,512,128]{2,1,0:T(8,128)(2,1)S(1)}) custom-call(f32[512,512]{1,0:T(8,128)S(1)} %get-tuple-element.114.x_ref, f32[512,512]{1,0:T(8,128)S(1)} %fusion.23.gate_ref, bf16[512,256]{1,0:T(8,128)(2,1)S(1)} %maximum_maximum_fusion.bc_ref, ...), custom_call_target="tpu_custom_call" | custom-call | tf_op jit(solution)/shard_map/pallas_call | solution.py:496
  76.1 3.7 %fusion.98 = (bf16[512,1024]{1,0:T(8,128)(2,1)}, f32[512]{0:T(512)S(1)}) fusion(bf16[512,1024]{1,0:T(8,128)(2,1)S(1)} %copy-done.8, bf16[512,512]{1,0:T(8,128)(2,1)S(1)} %get-tuple-element.31, bf16[1024,1664]{1,0:T(8,128)(2,1)} %copy-done.1), kind=kOutput, calls=%fused_computation.191 | convolution fusion | flops 538967552 | bytes 3672064 | tf_op jit(solution)/shard_map/dot_general | solution.py:66
  79.8 1.1 reduce.3
  80.9 6.1 %shard_map.283 = f32[4,2,512]{2,1,0:T(2,128)S(1)} custom-call(f32[2,512]{1,0:T(2,128)S(1)} %pad_maximum_fusion.8.x_ref), custom_call_target="tpu_custom_call" | custom-call | tf_op jit(solution)/shard_map/pallas_call | solution.py:170
  87.4 2.4 %fusion.17 = f32[512,512]{1,0:T(8,128)S(1)} fusion(bf16[1024,1664]{1,0:T(8,128)(2,1)} %copy-done.1, bf16[512,1024]{1,0:T(8,128)(2,1)} %cot_ref.1, f32[512]{0:T(512)S(1)} %bitcast.118), kind=kOutput, calls=%fused_computation.47 | convolution fusion | flops 538443776 | bytes 3147776 | tf_op jit(solution)/shard_map/dot_general | solution.py:791
  89.8 1.6 multiply_reduce_fusion.1
  91.4 1.1 fusion.8
  92.4 1.0 copy-done.2
  93.9 1.6 shard_map.284
  95.5 0.8 copy-done.5
  96.7 1.2 fusion.40.end_ref
  98.0 0.9 copy-done.11
  99.0 1.0 copy-done.13
  99.9 0.9 copy-done.27
  100.9 9.9 %shard_map.285 = (f32[512,512]{1,0:T(8,128)S(1)}, f32[512,256]{1,0:T(8,128)S(1)}, f32[512,8]{1,0:T(8,128)S(1)}, f32[512,8]{1,0:T(8,128)S(1)}) custom-call(f32[512,512]{1,0:T(8,128)S(1)} %get-tuple-element.114.x_ref, f32[512,512]{1,0:T(8,128)S(1)} %copy-done.3, bf16[512,256]{1,0:T(8,128)(2,1)S(1)} %maximum_maximum_fusion.bc_ref, f32[512,8]{1,0:T(8,128)S(1)} %copy-done.13, ...), custom_call_target="tpu_custom_call" | custom-call | flops 40000000000 | bytes 8388608 | tf_op jit(solution)/shard_map/pallas_call | solution.py:632
  110.7 1.0 copy-done.16
  111.7 0.8 copy-done.17
  112.5 0.7 copy-done.19
  113.2 0.7 copy-done.20
  113.9 1.0 copy.86
  115.0 1.1 copy.87
  116.0 4.0 %multiply_reduce_fusion.4 = (f32[512]{0:T(512)S(1)}, f32[512]{0:T(512)S(1)}, f32[512]{0:T(512)S(1)}, f32[512]{0:T(512)S(1)}, f32[512]{0:T(512)S(1)}, /*index=5*/f32[512,512]{1,0:T(8,128)S(1)}) fusion(f32[512,512]{1,0:T(8,128)} %copy-done.29, f32[3,512]{1,0:T(4,128)S(1)} %collective-permute-done, f32[512,512]{1,0:T(8,128)} %get-tuple-element.115, ...), kind=kLoop, calls=%fused_computation.36 | loop fusion | flops 5502464 | bytes 4210688 | tf_op jit(solution)/shard_map/transpose(jvp())/reduce_sum | solution.py:53
  120.6 1.5 collective-permute-start.2
  122.2 1.5 pad_add_fusion
  123.9 1.8 convolution_convert_fusion
  125.8 1.8 convolution_convert_fusion.2
  127.6 3.3 %fusion.21 = f32[512,1024]{1,0:T(8,128)} fusion(bf16[512,512]{1,0:T(8,128)(2,1)S(1)} %copy-done.32, bf16[1024,1664]{1,0:T(8,128)(2,1)} %copy-done.1), kind=kOutput, calls=%fused_computation.51 | convolution fusion | flops 536870912 | bytes 3670016 | tf_op jit(solution)/shard_map/dot_general | solution.py:66
  131.2 3.1 %convolution_convert_fusion.1 = bf16[1024,512]{1,0:T(8,128)(2,1)} fusion(f32[515,512]{1,0:T(8,128)} %pad_add_fusion, f32[3,512]{1,0:T(4,128)S(1)} %collective-permute-done.2, bf16[512,1024]{1,0:T(8,128)(2,1)S(1)} %copy-done, f32[1024]{0:T(1024)S(1)} %copy-done.23, f32[512]{0:T(512)S(1)} %add_rsqrt_fusion), kind=kOutput, calls=%fused_computation.17 | convolution fusion | flops 540016640 | bytes 3158016 | tf_op jit(solution)/shard_map/dot_general | solution.py:72
  134.4 1.8 add_convert_fusion
  136.7 9.7 %shard_map.286 = bf16[4,256,128]{2,1,0:T(8,128)(2,1)S(1)} custom-call(bf16[4,256,128]{2,1,0:T(8,128)(2,1)S(1)} %pad_maximum_fusion.5.x_ref), custom_call_target="tpu_custom_call" | custom-call | tf_op jit(solution)/shard_map/pallas_call | solution.py:386
  147.1 1.3 collective-permute-start.3
  148.5 1.6 collective-permute-done.3
  150.2 1.4 fusion.43
  151.7 2.5 %fusion.3 = (f32[1024]{0:T(1024)S(1)}, bf16[512,1024]{1,0:T(8,128)(2,1)S(1)}) fusion(bf16[512,1024]{1,0:T(8,128)(2,1)S(1)} %copy-done, f32[512]{0:T(512)S(1)} %add_rsqrt_fusion, f32[512,1024]{1,0:T(8,128)S(1)} %fusion.43, f32[512,1024]{1,0:T(8,128)S(1)} %copy-done.28, bf16[1024,1664]{1,0:T(8,128)(2,1)} %copy-done.1, f32[515,512]{1,0:T(8,128)} %pad_add_fusion, ...), kind=kOutput, calls=%fused_computation.8 | convolution fusion | flops 541064192 | bytes 8400896 | tf_op jit(solution)/shard_map/dot_general | solution.py:66
  154.3 0.7 convolution_convert_fusion.3
  155.8 1.4 pad_maximum_fusion.grads_ref
  157.2 61.5 %shard_map.287 = (f32[128,1664]{1,0:T(8,128)S(1)}, f32[512,1024]{1,0:T(8,128)S(1)}, f32[40,128]{1,0:T(8,128)S(1)}, f32[8,128]{1,0:T(8,128)S(1)}) custom-call(bf16[1024,1664]{1,0:T(8,128)(2,1)S(1)} %pad_maximum_fusion.grads_ref, bf16[512,1024]{1,0:T(8,128)(2,1)S(1)} %get-tuple-element.119.part_ref, f32[40,128]{1,0:T(8,128)S(1)} %bitcast.95, ...), custom_call_target="tpu_custom_call" | custom-call | tf_op jit(solution)/shard_map/pallas_call | solution.py:333
  218.7 1.3 copy-done.6
  221.3 0.9 slice_bitcast_fusion
  222.2 0.8 copy.94
  223.0 0.7 copy.92
  226.8 2.3 copy.106
  229.1 1.3 copy.107
  (191 shorter events, 14.2 us)
Async XLA Ops:
  7.2 127.2 %reduce-scatter.2.cloned.1.call-start = ((), (), s32[]{:S(2)}) async-start(), calls=%async_computation.1 | async-start | bytes 1310720 | tf_op jit(solution)/shard_map/reduce_scatter | solution.py:779
  11.0 25.4 %copy-start = (bf16[512,1024]{1,0:T(8,128)(2,1)S(1)}, bf16[512,1024]{1,0:T(8,128)(2,1)}, u32[]{:S(2)}) copy-start(bf16[512,1024]{1,0:T(8,128)(2,1)} %tokens_ref.1) | copy-start | bytes 3145732
  11.0 27.1 %copy-start.23 = (f32[1024]{0:T(1024)S(1)}, f32[1024]{0:T(1024)}, u32[]{:S(2)}) copy-start(f32[1024]{0:T(1024)} %param.17) | copy-start | bytes 12292
  36.4 1.7 copy-start.1
  38.7 6.0 %copy-start.38 = (f32[512,128]{0,1:T(8,128)}, f32[512,128]{0,1:T(8,128)S(1)}, u32[]{:S(2)}) copy-start(f32[512,128]{0,1:T(8,128)S(1)} %fusion.45) | copy-start | bytes 786436
  38.8 5.8 %copy-start.43 = (f32[8]{0:T(128)S(1)}, f32[8]{0:T(128)}, u32[]{:S(2)}) copy-start(f32[8]{0:T(128)} %param.26) | copy-start | bytes 100
  38.8 11.9 %collective-permute-start.1 = (f32[3,64]{1,0:T(4,128)S(1)}, f32[3,64]{1,0:T(4,128)S(1)}, u32[]{:S(2)}, u32[]{:S(2)}) collective-permute-start(f32[3,64]{1,0:T(4,128)S(1)} %copy.99), channel_id=1, source_target_pairs={{0,4},{1,5},{2,6},{3,7},{8,12},{9,13},{10,14},{11,15},{16,20},{17,... | collective-permute-start | bytes 2312 | tf_op jit(solution)/shard_map/ppermute | solution.py:21
  43.2 1.5 copy-start.29
  43.2 17.4 %collective-permute-start = (f32[3,512]{1,0:T(4,128)S(1)}, f32[3,512]{1,0:T(4,128)S(1)}, u32[]{:S(2)}, u32[]{:S(2)}) collective-permute-start(f32[3,512]{1,0:T(4,128)S(1)} %slice.332), channel_id=1, source_target_pairs={{0,4},{1,5},{2,6},{3,7},{8,12},{9,13},{10,14},{11,15},{16,20},{17,... | collective-permute-start | bytes 18440 | tf_op jit(solution)/shard_map/ppermute | solution.py:21
  44.6 20.3 %copy-start.45 = (pred[512]{0:T(512)(128)(4,1)}, pred[512]{0:T(512)(128)(4,1)S(1)}, u32[]{:S(2)}) copy-start(pred[512]{0:T(512)(128)(4,1)S(1)} %fusion.77) | copy-start | bytes 1540
  44.8 2.1 slice-start
  44.8 2.3 copy-start.47
  44.8 2.3 copy-start.40
  44.9 2.3 copy-start.53
  44.9 5.1 %copy-start.48 = (f32[8]{0:T(128)S(1)}, f32[8]{0:T(128)}, u32[]{:S(2)}) copy-start(f32[8]{0:T(128)} %param.28) | copy-start | bytes 100
  44.9 5.8 %copy-start.51 = (f32[64]{0:T(128)S(1)}, f32[64]{0:T(128)}, u32[]{:S(2)}) copy-start(f32[64]{0:T(128)} %param.25) | copy-start | bytes 772
  47.1 13.4 %copy-start.30 = (f32[512,64]{1,0:T(8,128)}, f32[512,64]{1,0:T(8,128)S(1)}, u32[]{:S(2)}) copy-start(f32[512,64]{1,0:T(8,128)S(1)} %copy.100) | copy-start | bytes 393220
  47.1 13.5 %copy-start.41 = (f32[64]{0:T(128)}, f32[64]{0:T(128)S(1)}, u32[]{:S(2)}) copy-start(f32[64]{0:T(128)S(1)} %get-tuple-element.168) | copy-start | bytes 772
  47.2 0.9 copy-start.49
  64.9 5.8 %copy-start.22 = (f32[512]{0:T(512)S(1)}, f32[512]{0:T(512)}, u32[]{:S(2)}) copy-start(f32[512]{0:T(512)} %param.29) | copy-start | bytes 6148
  68.1 0.8 copy-start.4
  69.3 6.7 %copy-start.8 = (bf16[512,1024]{1,0:T(8,128)(2,1)S(1)}, bf16[512,1024]{1,0:T(8,128)(2,1)}, u32[]{:S(2)}) copy-start(bf16[512,1024]{1,0:T(8,128)(2,1)} %cot_ref.1) | copy-start | bytes 3145732
  70.7 1.0 copy-start.10
  71.6 0.9 copy-start.12
  76.0 3.8 %copy-start.14 = (f32[512,512]{1,0:T(8,128)}, f32[512,512]{1,0:T(8,128)S(1)}, u32[]{:S(2)}) copy-start(f32[512,512]{1,0:T(8,128)S(1)} %get-tuple-element.32) | copy-start | bytes 3145732
  76.1 3.7 %copy-start.21 = (f32[512,1]{1,0:T(8,128)}, f32[512,1]{1,0:T(8,128)S(1)}, u32[]{:S(2)}) copy-start(f32[512,1]{1,0:T(8,128)S(1)} %get-tuple-element.30) | copy-start | bytes 6148
  76.1 3.7 %copy-start.24 = (bf16[512,512]{1,0:T(8,128)(2,1)}, bf16[512,512]{1,0:T(8,128)(2,1)S(1)}, u32[]{:S(2)}) copy-start(bf16[512,512]{1,0:T(8,128)(2,1)S(1)} %get-tuple-element.31) | copy-start | bytes 1572868
  76.1 3.7 %copy-start.26 = (bf16[2,512,128]{2,1,0:T(8,128)(2,1)}, bf16[2,512,128]{2,1,0:T(8,128)(2,1)S(1)}, u32[]{:S(2)}) copy-start(bf16[2,512,128]{2,1,0:T(8,128)(2,1)S(1)} %get-tuple-element.33.kept_ref) | copy-start | bytes 786436
  87.1 139.7 %all-gather.2.cloned.1.call-start = ((), (), s32[]{:S(2)}) async-start(), calls=%async_computation.2 | async-start | bytes 1310720 | tf_op jit(solution)/shard_map/all_gather | solution.py:821
  87.3 2.4 %copy-start.15 = (f32[512,512]{1,0:T(8,128)S(1)}, f32[512,512]{1,0:T(8,128)}, u32[]{:S(2)}) copy-start(f32[512,512]{1,0:T(8,128)} %copy-done.14) | copy-start | bytes 3145732
  89.8 1.6 copy-start.46
  92.4 1.0 copy-start.2
  93.7 4.3 %copy-start.3 = (f32[512,512]{1,0:T(8,128)S(1)}, f32[512,512]{1,0:T(8,128)}, u32[]{:S(2)}) copy-start(f32[512,512]{1,0:T(8,128)} %copy-done.2) | copy-start | bytes 3145732
  95.5 0.8 copy-start.5
  98.0 1.0 copy-start.11
  99.0 1.0 copy-start.13
  99.9 1.0 copy-start.27
  110.7 1.0 copy-start.16
  111.7 0.8 copy-start.17
  112.5 0.7 copy-start.19
  113.2 0.7 copy-start.20
  120.6 10.6 %collective-permute-start.2 = (f32[3,512]{1,0:T(4,128)S(1)}, f32[3,512]{1,0:T(4,128)S(1)}, u32[]{:S(2)}, u32[]{:S(2)}) collective-permute-start(f32[3,512]{1,0:T(4,128)S(1)} %pad_add_fusion.2), channel_id=1, source_target_pairs={{4,0},{5,1},{6,2},{7,3},{12,8},{13,9},{14,10},{15,11},{20,16},{21,... | collective-permute-start | bytes 18440 | tf_op jit(solution)/shard_map/ppermute | solution.py:21
  122.1 1.5 copy-start.39
  122.2 1.5 copy-start.44
  122.2 1.5 copy-start.50
  122.2 1.8 copy-start.9
  122.2 1.8 copy-start.25
  123.7 2.1 copy-start.32
  131.0 19.2 %copy-start.36 = (bf16[512,8]{1,0:T(8,128)(2,1)}, bf16[512,8]{1,0:T(8,128)(2,1)S(1)}, u32[]{:S(2)}) copy-start(bf16[512,8]{1,0:T(8,128)(2,1)S(1)} %copy.88) | copy-start | bytes 24580
  131.2 5.0 %copy-start.18 = (f32[512,256]{1,0:T(8,128)S(1)}, f32[512,256]{1,0:T(8,128)}, u32[]{:S(2)}) copy-start(f32[512,256]{1,0:T(8,128)} %copy-done.17) | copy-start | bytes 1572868
  136.2 10.3 %copy-start.31 = (f32[512,64]{1,0:T(8,128)S(1)}, f32[512,64]{1,0:T(8,128)}, u32[]{:S(2)}) copy-start(f32[512,64]{1,0:T(8,128)} %copy-done.30) | copy-start | bytes 393220
  136.2 10.3 %copy-start.33 = (f32[512,64]{1,0:T(8,128)S(1)}, f32[512,64]{1,0:T(8,128)}, u32[]{:S(2)}) copy-start(f32[512,64]{1,0:T(8,128)} %get-tuple-element.113) | copy-start | bytes 393220
  136.4 10.5 %copy-start.42 = (f32[64]{0:T(128)S(1)}, f32[64]{0:T(128)}, u32[]{:S(2)}) copy-start(f32[64]{0:T(128)} %copy-done.41) | copy-start | bytes 772
  146.9 3.3 %copy-start.52 = (bf16[128]{0:T(256)(128)(2,1)S(1)}, bf16[128]{0:T(256)(128)(2,1)}, u32[]{:S(2)}) copy-start(bf16[128]{0:T(256)(128)(2,1)} %pad.81.clone) | copy-start | bytes 772
  147.1 3.1 %collective-permute-start.3 = (f32[3,64]{1,0:T(4,128)S(1)}, f32[3,64]{1,0:T(4,128)S(1)}, u32[]{:S(2)}, u32[]{:S(2)}) collective-permute-start(f32[3,64]{1,0:T(4,128)S(1)} %pad_add_fusion.3), channel_id=1, source_target_pairs={{4,0},{5,1},{6,2},{7,3},{12,8},{13,9},{14,10},{15,11},{20,16},{21,... | collective-permute-start | bytes 2312 | tf_op jit(solution)/shard_map/ppermute | solution.py:21
  148.5 3.1 %copy-start.28 = (f32[512,1024]{1,0:T(8,128)S(1)}, f32[512,1024]{1,0:T(8,128)}, u32[]{:S(2)}) copy-start(f32[512,1024]{1,0:T(8,128)} %fusion.21) | copy-start | bytes 6291460
  151.6 2.6 %copy-start.37 = (bf16[512,8]{1,0:T(8,128)(2,1)S(1)}, bf16[512,8]{1,0:T(8,128)(2,1)}, u32[]{:S(2)}) copy-start(bf16[512,8]{1,0:T(8,128)(2,1)} %copy-done.36) | copy-start | bytes 24580
  154.3 1.2 copy-start.34
  154.3 1.5 copy-start.35
  218.7 1.3 copy-start.6
  221.3 7.8 %copy-start.7 = (f32[512,1024]{1,0:T(8,128)S(1)}, f32[512,1024]{1,0:T(8,128)}, u32[]{:S(2)}) copy-start(f32[512,1024]{1,0:T(8,128)} %copy-done.6) | copy-start | bytes 6291460
Sparse Core Ops, SparseCore 0:
  87.2 27.3 reduce-scatter.1
  148.6 49.1 all-gather.1
